TPU v7x, 128 devices: a whole 4x4x4 slice. The times are simulated.
128 devices in a mesh: row: 16 (over x, z), col: 8 (over y, core).
Axes of the slice: x: 4, y: 4, z: 4, core: 2. Of those that a mesh axis runs over, the one named last changes fastest.
Arguments:
- attn: bfloat16 [2048, 16384], P('col', 'row'), may hold values from -6 to 6
- grad_out: bfloat16 [2048, 16384], P('row', 'col'), may hold values from -0.119628906 to 0.119628906
- weight: bfloat16 [16384, 16384], P('row', 'col'), may hold values from -2.09375 to 2.09375
- momentum: bfloat16 [16384, 16384], P('row', 'col'), may hold values from -3 to 3
Outputs:
- grad_in: bfloat16 [2048, 16384], P('col', 'row')
- new_weight: bfloat16 [16384, 16384], P('row', 'col')
- new_momentum: bfloat16 [16384, 16384], P('row', 'col')
All inputs are finite; a program needn't handle non-finite values.
Results may differ from a plain program's by a relative error of at most 0.014.
Values may be sent and summed in bfloat16 or wider, within the bound.
A program may use at most 128 MiB of HBM per device.

v0:
```python
import jax
import jax.numpy as jnp
from jax import lax
from jax.sharding import PartitionSpec as P


def shards(attn, grad_out, weight, momentum):
    contract_rows = (((0,), (0,)), ((), ()))
    contract_cols = (((1,), (1,)), ((), ()))
    grads_all = lax.all_gather(grad_out, "row", axis=0, tiled=True)
    rows_here = grads_all
    grad_w = lax.dot_general(
        lax.all_gather(attn, "col", axis=0, tiled=True),
        rows_here,
        contract_rows,
        preferred_element_type=jnp.float32,
    )
    rows_here = grads_all
    grad_in = lax.psum_scatter(
        lax.dot_general(
            rows_here, weight, contract_cols, preferred_element_type=jnp.float32
        ).astype(jnp.bfloat16),
        "col",
        scatter_dimension=0,
        tiled=True,
    )
    mom = 0.9 * momentum.astype(jnp.float32) + grad_w
    new_weight = (weight.astype(jnp.float32) - 0.25 * mom).astype(jnp.bfloat16)
    return (grad_in, new_weight, mom.astype(jnp.bfloat16))


def solution(mesh):
    in_specs = (P("col", "row"), P("row", "col"), P("row", "col"), P("row", "col"))
    out_specs = (P("col", "row"), P("row", "col"), P("row", "col"))
    return jax.shard_map(shards, mesh=mesh, in_specs=in_specs, out_specs=out_specs, check_vma=False)
```

profile of v0, /device:TPU:0, one launch (start us, length us, event | category | flops | bytes accessed | tf_op | source)
XLA Modules:
  0.0 164.3 jit_solution(2336899763222875752)
XLA Ops:
  7.2 0.0 all-gather.3.cloned.1.call-start
  7.2 0.7 all-gather.3.cloned.1.call-update
  7.9 0.0 all-gather.5.cloned.1.call-start
  7.9 0.7 all-gather.5.cloned.1.call-update
  8.6 0.0 reduce-scatter.2.cloned.1.call-start
  8.7 74.9 %all-gather.3.cloned.1.call-done = bf16[2048,2048]{1,0:T(8,128)(2,1)} async-done(((bf16[128,2048]{1,0:T(8,128)(2,1)}), bf16[2048,2048]{1,0:T(8,128)(2,1)}) %all-gather.3.cloned.1.call-update) | async-done | bytes 8388624 | tf_op jit(solution)/shard_map/all_gather | solution.py:10
  83.6 13.8 %convolution_convert_fusion = bf16[2048,1024]{1,0:T(8,128)(2,1)} fusion(bf16[2048,2048]{1,0:T(8,128)(2,1)} %all-gather.3.cloned.1.call-done, bf16[1024,2048]{1,0:T(8,128)(2,1)} %param.6), kind=kOutput, calls=%fused_computation.3 | convolution fusion | flops 8592031744 | bytes 16777216 | tf_op jit(solution)/shard_map/dot_general | solution.py:20
  97.4 0.0 reduce-scatter.2.cloned.1.call-update
  97.4 19.5 %all-gather.5.cloned.1.call-done = bf16[2048,1024]{1,0:T(8,128)(2,1)} async-done(((bf16[256,1024]{1,0:T(8,128)(2,1)}), bf16[2048,1024]{1,0:T(8,128)(2,1)}) %all-gather.5.cloned.1.call-update) | async-done | bytes 4194320 | tf_op jit(solution)/shard_map/all_gather | solution.py:13
  117.0 17.7 %fusion = (bf16[1024,2048]{1,0:T(8,128)(2,1)}, bf16[1024,2048]{1,0:T(8,128)(2,1)}) fusion(bf16[1024,2048]{1,0:T(8,128)(2,1)} %param.7, bf16[1024,2048]{1,0:T(8,128)(2,1)} %param.6, bf16[2048,1024]{1,0:T(8,128)(2,1)} %all-gather.5.cloned.1.call-done, bf16[2048,2048]{1,0:T(8,128)(2,1)} %all-gather.3.cloned.1.call-done), kind=kOutput, calls=%fused_computation.2 | convolution fusion | flops 8606711808 | bytes 29360128 | tf_op jit(solution)/shard_map/dot_general | solution.py:12
  134.7 23.1 %reduce-scatter.2.cloned.1.call-done = bf16[256,1024]{1,0:T(8,128)(2,1)} async-done(((bf16[2048,1024]{1,0:T(8,128)(2,1)}), bf16[256,1024]{1,0:T(8,128)(2,1)}) %reduce-scatter.2.cloned.1.call-update) | async-done | bytes 524304 | tf_op jit(solution)/shard_map/reduce_scatter | solution.py:19
Async XLA Ops:
  7.2 76.4 %all-gather.3.cloned.1.call-start = ((), (), s32[]{:S(2)}) async-start(), calls=%async_computation.1 | async-start | bytes 8912896 | tf_op jit(solution)/shard_map/all_gather | solution.py:10
  7.9 109.1 %all-gather.5.cloned.1.call-start = ((), (), s32[]{:S(2)}) async-start(), calls=%async_computation.3 | async-start | bytes 4718592 | tf_op jit(solution)/shard_map/all_gather | solution.py:13
  8.6 149.2 %reduce-scatter.2.cloned.1.call-start = ((), (), s32[]{:S(2)}) async-start(), calls=%async_computation.2 | async-start | bytes 4718592 | tf_op jit(solution)/shard_map/reduce_scatter | solution.py:19
Sparse Core Ops, SparseCore 0:
  10.1 73.4 all-gather.2
  85.3 31.6 all-gather.4
  119.9 37.8 reduce-scatter.1
where the time goes:
time: 164 us
  waiting for transfers between devices  119 us (73%)
  matrix products  31.6 us (19%)
  between operations  13.7 us (8%)
    all_gather x1, waiting for transfers between devices, shards(): grads_all = lax.all_gather(grad_out, 'row', axis=0, tiled=True)  74.9 us
    reduce_scatter x1, waiting for transfers between devices, shards(): lax.psum_scatter(lax.dot_general(rows_here, weight, contract_cols, prefer...  23.1 us
    all_gather x1, waiting for transfers between devices, shards(): lax.all_gather(attn, 'col', axis=0, tiled=True)  19.5 us
    dot_general x1, matrix products, shards(): lax.dot_general(lax.all_gather(attn, 'col', axis=0, tiled=True), rows_her...  17.7 us
    dot_general x1, matrix products, shards(): lax.dot_general(rows_here, weight, contract_cols, preferred_element_type=...  13.8 us
  transfers between devices with their start and end apart: 3, of which 3 were waited for; matrix products, arithmetic and copies ran while one was open for 19% of the time, Pallas kernels for 0%

commit v1 on v0

--- a/solution.py
+++ b/solution.py
@@ -7,7 +7,8 @@
 def shards(attn, grad_out, weight, momentum):
     contract_rows = (((0,), (0,)), ((), ()))
     contract_cols = (((1,), (1,)), ((), ()))
-    grads_all = lax.all_gather(grad_out, "row", axis=0, tiled=True)
+    repeated = jnp.stack([grad_out] * lax.axis_size("row"))
+    grads_all = jnp.concatenate(lax.all_to_all(repeated, "row", 0, 0), axis=0)
     rows_here = grads_all
     grad_w = lax.dot_general(
         lax.all_gather(attn, "col", axis=0, tiled=True),

time: 164 us -> 231 us (1.41)
  waiting for transfers between devices: 119 us -> 172 us
  starting transfers between devices: 0.11 us -> 8.12 us
  local copies, waits for them, and re-layouts: 0 us -> 5.34 us
    all_to_all x0 -> x1, waiting for transfers between devices: none -> 147 us  [shards(): grads_all = jnp.concatenate(lax.all_to_all(repeated, 'row', 0, 0), axis=0)]
    all_gather x1 -> x0, waiting for transfers between devices: 74.9 us -> none  [shards(): grads_all = lax.all_gather(grad_out, 'row', axis=0, tiled=True)]
    all_gather x1, waiting for transfers between devices: 19.5 us -> 0.02 us  [shards(): lax.all_gather(attn, 'col', axis=0, tiled=True)]
    all_to_all x0 -> x1, starting transfers between devices: none -> 8.04 us  [shards(): grads_all = jnp.concatenate(lax.all_to_all(repeated, 'row', 0, 0), axis=0)]
    another operation x0 -> x1, local copies, waits for them, and re-layouts: none -> 5.34 us  [shards(): repeated = jnp.stack([grad_out] * lax.axis_size('row'))]
  transfers between devices with their start and end apart: 3 -> 3, of which waited for: 3 -> 2; matrix products, arithmetic and copies ran while one was open for 19% -> 14% of each run, Pallas kernels for 0% -> 0%
where the time goes in v1:
time: 231 us
  waiting for transfers between devices  172 us (74%)
  matrix products  31.6 us (14%)
  between operations  14.1 us (6%)
  starting transfers between devices  8.12 us (4%)
  local copies, waits for them, and re-layouts  5.34 us (2%)
    all_to_all x1, waiting for transfers between devices, shards(): grads_all = jnp.concatenate(lax.all_to_all(repeated, 'row', 0, 0), axis=0)  147 us
    reduce_scatter x1, waiting for transfers between devices, shards(): lax.psum_scatter(lax.dot_general(rows_here, weight, contract_cols, prefer...  24.1 us
    dot_general x1, matrix products, shards(): lax.dot_general(lax.all_gather(attn, 'col', axis=0, tiled=True), rows_her...  17.7 us
    dot_general x1, matrix products, shards(): lax.dot_general(rows_here, weight, contract_cols, preferred_element_type=...  13.9 us
    all_to_all x1, starting transfers between devices, shards(): grads_all = jnp.concatenate(lax.all_to_all(repeated, 'row', 0, 0), axis=0)  8.04 us
    another operation x1, local copies, waits for them, and re-layouts, shards(): repeated = jnp.stack([grad_out] * lax.axis_size('row'))  5.34 us
  transfers between devices with their start and end apart: 3, of which 2 were waited for; matrix products, arithmetic and copies ran while one was open for 14% of the time, Pallas kernels for 0%

profile of v1, /device:TPU:0, one launch (start us, length us, event | category | flops | bytes accessed | tf_op | source)
XLA Modules:
  0.0 230.7 jit_solution(1454349569333646557)
XLA Ops:
  7.2 5.3 %stack.2 = bf16[16,128,2048]{2,1,0:T(8,128)(2,1)} broadcast(bf16[128,2048]{1,0:T(8,128)(2,1)} %param.5), dimensions={1,2} | broadcast | bytes 8912896 | tf_op jit(solution)/shard_map/stack | solution.py:10
  12.5 8.0 %all-to-all-start = ((bf16[16,128,2048]{2,1,0:T(8,128)(2,1)}), bf16[16,128,2048]{2,1,0:T(8,128)(2,1)}, u32[]{:S(2)}, u32[]{:S(2)}) async-start(bf16[16,128,2048]{2,1,0:T(8,128)(2,1)} %stack.2), calls=%async_computation | async-start | bytes 16777216 | tf_op jit(solution)/shard_map/all_to_all | solution.py:11
  20.5 0.0 all-gather.2.cloned.1.call-start
  20.6 0.7 all-gather.2.cloned.1.call-update
  21.3 0.0 reduce-scatter.2.cloned.1.call-start
  21.3 146.8 %all-to-all-done = bf16[16,128,2048]{2,1,0:T(8,128)(2,1)} async-done(((bf16[16,128,2048]{2,1,0:T(8,128)(2,1)}), bf16[16,128,2048]{2,1,0:T(8,128)(2,1)}, u32[]{:S(2)}, u32[]{:S(2)}) %all-to-all-start) | async-done | bytes 8388640 | tf_op jit(solution)/shard_map/all_to_all | solution.py:11
  168.1 13.9 %convolution_convert_fusion = bf16[2048,1024]{1,0:T(8,128)(2,1)} fusion(bf16[2048,2048]{1,0:T(8,128)(2,1)} %bitcast, bf16[1024,2048]{1,0:T(8,128)(2,1)} %param.6), kind=kOutput, calls=%fused_computation.3 | convolution fusion | flops 8592031744 | bytes 16777216 | tf_op jit(solution)/shard_map/dot_general | solution.py:21
  182.0 0.0 reduce-scatter.2.cloned.1.call-update
  182.0 0.0 all-gather.2.cloned.1.call-done
  182.0 17.7 %fusion = (bf16[1024,2048]{1,0:T(8,128)(2,1)}, bf16[1024,2048]{1,0:T(8,128)(2,1)}) fusion(bf16[1024,2048]{1,0:T(8,128)(2,1)} %param.7, bf16[1024,2048]{1,0:T(8,128)(2,1)} %param.6, bf16[2048,1024]{1,0:T(8,128)(2,1)} %all-gather.2.cloned.1.call-done, bf16[2048,2048]{1,0:T(8,128)(2,1)} %bitcast), kind=kOutput, calls=%fused_computation.2 | convolution fusion | flops 8606711808 | bytes 29360128 | tf_op jit(solution)/shard_map/dot_general | solution.py:13
  199.8 24.1 %reduce-scatter.2.cloned.1.call-done = bf16[256,1024]{1,0:T(8,128)(2,1)} async-done(((bf16[2048,1024]{1,0:T(8,128)(2,1)}), bf16[256,1024]{1,0:T(8,128)(2,1)}) %reduce-scatter.2.cloned.1.call-update) | async-done | bytes 524304 | tf_op jit(solution)/shard_map/reduce_scatter | solution.py:20
Async XLA Ops:
  12.5 155.6 %all-to-all-start = ((bf16[16,128,2048]{2,1,0:T(8,128)(2,1)}), bf16[16,128,2048]{2,1,0:T(8,128)(2,1)}, u32[]{:S(2)}, u32[]{:S(2)}) async-start(bf16[16,128,2048]{2,1,0:T(8,128)(2,1)} %stack.2), calls=%async_computation | async-start | bytes 16777216 | tf_op jit(solution)/shard_map/all_to_all | solution.py:11
  20.5 161.5 %all-gather.2.cloned.1.call-start = ((), (), s32[]{:S(2)}) async-start(), calls=%async_computation.3 | async-start | bytes 4718592 | tf_op jit(solution)/shard_map/all_gather | solution.py:14
  21.3 202.6 %reduce-scatter.2.cloned.1.call-start = ((), (), s32[]{:S(2)}) async-start(), calls=%async_computation.2 | async-start | bytes 4718592 | tf_op jit(solution)/shard_map/reduce_scatter | solution.py:20
Sparse Core Ops, SparseCore 0:
  23.1 33.7 all-gather.1
  182.1 41.7 reduce-scatter.1
